TPU v7x, 32 devices: a whole 2x2x4 slice. The times are simulated.
32 devices in a mesh: facet: 4 (over z), col: 8 (over y, x, core).
Axes of the slice: x: 2, y: 2, z: 4, core: 2. Of those that a mesh axis runs over, the one named last changes fastest.
Arguments:
- facets: bfloat16 [4, 64, 2, 128], P('facet', 'col'), may hold values from -6 to 6
- sub_offsets: int32 [8, 4], P('col'), may hold values from 0 to 8191
- col_offsets: int32 [8], P('col'), may hold values from 0 to 8191
- screen_index: int32 [8, 4], P('col', 'facet'), may hold values from 0 to 3
- screens: float32 [4, 2, 256, 256], replicated, may hold values from -6 to 6
Outputs:
- facets_out: float32 [4, 64, 2, 128], P('facet', 'col')
All inputs are finite; a program needn't handle non-finite values.
Results may differ from a plain program's by a relative error of at most 0.0056.
Values may be sent and summed in bfloat16 or wider, within the bound.
No kernel may reach another device: no remote copies, remote signals or barrier semaphores. Data moves between devices by JAX's collectives and lax.ppermute only.
A program may use at most 64 MiB of HBM per device.

v0:
```python
import math
import jax
import jax.numpy as jnp
from jax import lax
from jax.sharding import PartitionSpec as P

XC = 64
XS = 256
SLAB = 128
NPAD = 8192


def phase_pair(numerator, period, direction, factor):
    angles = direction * 2.0 * math.pi / period * numerator.astype(jnp.float32)
    return (
        (jnp.cos(angles) * factor).astype(jnp.bfloat16),
        (jnp.sin(angles) * factor).astype(jnp.bfloat16),
    )


def embed_table(facet_ids):
    column = jnp.arange(XS, dtype=jnp.int32)
    within = jnp.arange(XC, dtype=jnp.int32)
    product = column[None, :, None] * (within[None, None, :] + 7 * facet_ids[:, None, None]) % XS
    return phase_pair(product, XS, 1.0, 1.0 / math.sqrt(XS))


def column_table(offset):
    position = jnp.arange(SLAB, dtype=jnp.int32)
    frequency = (offset + jnp.arange(XC, dtype=jnp.int32)) % NPAD
    product = position[:, None] * frequency[None, :] % NPAD
    return phase_pair(product, NPAD, -1.0, 1.0 / math.sqrt(SLAB))


def row_table(offsets, row_ids, height):
    frequency = (offsets[:, None] + jnp.arange(XC, dtype=jnp.int32)[None, :]) % NPAD
    frequency = frequency.reshape(frequency.shape + (1,) * row_ids.ndim)
    product = frequency * (row_ids % NPAD) % NPAD
    return phase_pair(product, NPAD, -1.0, 1.0 / math.sqrt(height))


def general_dot(first_op, second_op, contract):
    numbers = ((contract[0], contract[1]), ((), ()))
    return lax.dot_general(first_op, second_op, numbers, preferred_element_type=jnp.float32)


def complex_dot(first_op, second_op, contract):
    real_part = general_dot(first_op[0], second_op[0], contract) - general_dot(
        first_op[1], second_op[1], contract
    )
    imag_part = general_dot(first_op[0], second_op[1], contract) + general_dot(
        first_op[1], second_op[0], contract
    )
    return (real_part, imag_part)


def complex_einsum(form, first_op, second_op):

    def single(left_part, right_part):
        return jnp.einsum(form, left_part, right_part, preferred_element_type=jnp.float32)

    real_part = single(first_op[0], second_op[0]) - single(first_op[1], second_op[1])
    imag_part = single(first_op[0], second_op[1]) + single(first_op[1], second_op[0])
    return (real_part, imag_part)


def round_pair(values):
    return (values[0].astype(jnp.bfloat16), values[1].astype(jnp.bfloat16))


def body(facets, sub_offsets, col_offsets, screen_index, screens):
    facet_now = lax.axis_index("facet")
    facet_count = lax.axis_size("facet")
    column_count = lax.axis_size("col")
    local_rows = facets.shape[1]
    total_rows = local_rows * column_count
    subgrid_count = sub_offsets.shape[1]
    across = column_table(col_offsets[0])
    row_ids = facet_now * total_rows + jnp.arange(total_rows, dtype=jnp.int32)
    row_phase = row_table(sub_offsets[0], row_ids, total_rows)
    row_flat = (
        row_phase[0].reshape(subgrid_count * XC, total_rows),
        row_phase[1].reshape(subgrid_count * XC, total_rows),
    )
    embedding = embed_table(jnp.arange(facet_count, dtype=jnp.int32))
    adjoint_embed = (embedding[0], -embedding[1])
    whole_slab = lax.all_gather(facets[0], "col", axis=0, tiled=True)
    spread = round_pair(complex_dot((whole_slab[:, 0], whole_slab[:, 1]), across, ((1,), (0,))))
    block_phase = (row_flat[0], row_flat[1])
    summand = complex_dot(block_phase, spread, ((1,), (0,)))
    contrib_real = summand[0]
    contrib_imag = summand[1]
    contributions = jnp.stack(
        [contrib_real.reshape(subgrid_count, XC, XC), contrib_imag.reshape(subgrid_count, XC, XC)],
        axis=1,
    ).astype(jnp.bfloat16)
    outgoing = contributions.reshape(facet_count, subgrid_count // facet_count, 2, XC, XC)
    received = lax.all_to_all(outgoing, "facet", split_axis=0, concat_axis=0, tiled=True)
    factor = 1.0 / math.sqrt(received.shape[0])
    halfway = round_pair(
        complex_einsum("fkuv,fav->fkua", (received[:, :, 0], received[:, :, 1]), embedding)
    )
    subgrid = complex_einsum("fau,fkub->kab", embedding, halfway)
    subgrids = jnp.stack([subgrid[0] * factor, subgrid[1] * factor], axis=1)
    gain_maps = jnp.take(screens, screen_index[0], axis=0)
    sub_real = subgrids[:, 0]
    sub_imag = subgrids[:, 1]
    gain_real = gain_maps[:, 0]
    gain_imag = gain_maps[:, 1]
    screened = jnp.stack(
        [sub_real * gain_real - sub_imag * gain_imag, sub_real * gain_imag + sub_imag * gain_real],
        axis=1,
    ).astype(jnp.bfloat16)
    inner = round_pair(
        complex_einsum("fau,kab->fkub", adjoint_embed, (screened[:, 0], screened[:, 1]))
    )
    returned = round_pair(complex_einsum("fkub,fbv->fkuv", inner, adjoint_embed))
    going_back = jnp.stack([returned[0], returned[1]], axis=2)
    arrived = lax.all_to_all(going_back, "facet", split_axis=0, concat_axis=0, tiled=True)
    flat_parts = (
        arrived[:, :, 0].reshape(subgrid_count * XC, XC),
        arrived[:, :, 1].reshape(subgrid_count * XC, XC),
    )
    conj_rows = (row_flat[0], -row_flat[1])
    conj_across = (across[0], -across[1])
    block_phase = (conj_rows[0], conj_rows[1])
    slab_rows = round_pair(complex_dot(block_phase, flat_parts, ((0,), (0,))))
    summand = complex_dot(slab_rows, conj_across, ((1,), (1,)))
    summed = lax.psum_scatter(
        jnp.stack([summand[0], summand[1]], axis=1), "col", scatter_dimension=0, tiled=True
    )
    factor = 1.0 / math.sqrt(column_count * subgrid_count)
    return (summed * factor)[None]


def solution(mesh):
    return jax.shard_map(
        body,
        mesh=mesh,
        in_specs=(P("facet", "col", None, None), P("col", None), P("col"), P("col", "facet"), P()),
        out_specs=P("facet", "col", None, None),
        check_vma=False,
    )
```

profile of v0, /device:TPU:0, one launch (start us, length us, event | category | flops | bytes accessed | tf_op | source)
XLA Modules:
  0.0 103.0 jit_solution(15256467704068832730)
XLA Ops:
  7.4 0.7 copy.23
  8.0 10.3 %all-gather = bf16[1,64,2,128]{3,1,2,0:T(8,128)(2,1)S(1)} all-gather(bf16[1,8,2,128]{3,1,2,0:T(8,128)(2,1)S(1)} %copy.23), channel_id=2, replica_groups=mesh['facet'=4,'col'=8] {'col'}, dimensions={1}, use_global_device_ids=true | all-gather | bytes 36864 | tf_op jit(solution)/shard_map/all_gather | solution.py:87
  19.7 0.7 iota_add_fusion.1
  20.9 0.7 fusion.47
  21.6 0.7 fusion.48
  22.3 0.7 fusion.13
  23.1 0.7 fusion.12
  24.0 0.8 reshape.305
  24.8 4.9 %all-to-all-start = ((bf16[4,2,4096]{2,1,0:T(2,128)(2,1)}), bf16[4,2,4096]{2,1,0:T(2,128)(2,1)S(1)}, u32[]{:S(2)}, u32[]{:S(2)}) async-start(bf16[4,2,4096]{2,1,0:T(2,128)(2,1)} %reshape.305), calls=%async_computation | async-start | bytes 131072 | tf_op jit(solution)/shard_map/all_to_all | solution.py:98
  30.7 1.1 %multiply_convert_fusion.1 = bf16[4,256,64]{1,2,0:T(8,128)(2,1)S(1)} fusion(s32[4,64]{1,0:T(4,128)S(1)} %iota_add_fusion), kind=kLoop, calls=%fused_computation.50 | loop fusion | flops 1048576 | bytes 132096 | tf_op jit(solution)/shard_map/convert_element_type | solution.py:16
  31.8 1.1 %fusion.33 = bf16[4,256,64]{1,2,0:T(8,128)(2,1)S(1)} fusion(s32[4,64]{1,0:T(4,128)S(1)} %iota_add_fusion), kind=kLoop, calls=%fused_computation.68 | loop fusion | flops 1245184 | bytes 132096 | tf_op jit(solution)/shard_map/neg | solution.py:86
  32.8 2.5 %all-to-all-done = bf16[4,2,4096]{2,1,0:T(2,128)(2,1)S(1)} async-done(((bf16[4,2,4096]{2,1,0:T(2,128)(2,1)}), bf16[4,2,4096]{2,1,0:T(2,128)(2,1)S(1)}, u32[]{:S(2)}, u32[]{:S(2)}) %all-to-all-start) | async-done | bytes 65568 | tf_op jit(solution)/shard_map/all_to_all | solution.py:98
  35.5 1.6 %fusion.34 = f32[4,64,256]{2,1,0:T(8,128)S(1)} fusion(s32[4,64]{1,0:T(4,128)S(1)} %iota_add_fusion, bf16[4,1,2,64,64]{4,3,2,1,0:T(8,128)(2,1)S(1)} %reshape.306), kind=kOutput, calls=%fused_computation.69 | convolution fusion | flops 9437184 | bytes 329728 | tf_op jit(solution)/shard_map/fkuv,fav->fkua/dot_general | solution.py:60
  37.2 1.4 %fusion.36 = f32[4,64,256]{2,1,0:T(8,128)S(1)} fusion(s32[4,64]{1,0:T(4,128)S(1)} %iota_add_fusion, bf16[4,1,2,64,64]{4,3,2,1,0:T(8,128)(2,1)S(1)} %reshape.306), kind=kOutput, calls=%fused_computation.71 | convolution fusion | flops 9437184 | bytes 329728 | tf_op jit(solution)/shard_map/fkuv,fav->fkua/dot_general | solution.py:60
  38.6 1.2 %fusion.7 = bf16[4,64,256]{2,1,0:T(8,128)(2,1)S(1)} fusion(f32[4,64,256]{2,1,0:T(8,128)S(1)} %fusion.34, s32[4,64]{1,0:T(4,128)S(1)} %iota_add_fusion, bf16[4,1,2,64,64]{4,3,2,1,0:T(8,128)(2,1)S(1)} %reshape.306), kind=kOutput, calls=%fused_computation.13 | convolution fusion | flops 9568256 | bytes 460800 | tf_op jit(solution)/shard_map/fkuv,fav->fkua/dot_general | solution.py:60
  39.8 1.2 %convolution_bitcast_fusion.2 = f32[256,256]{1,0:T(8,128)S(1)} fusion(bf16[4,64,256]{2,1,0:T(8,128)(2,1)S(1)} %fusion.7, s32[4,64]{1,0:T(4,128)S(1)} %iota_add_fusion), kind=kOutput, calls=%fused_computation.4 | convolution fusion | flops 34603008 | bytes 394240 | tf_op jit(solution)/shard_map/fau,fkub->kab/dot_general | solution.py:60
  41.0 1.2 %fusion.6 = bf16[4,64,256]{2,1,0:T(8,128)(2,1)S(1)} fusion(f32[4,64,256]{2,1,0:T(8,128)S(1)} %fusion.36, s32[4,64]{1,0:T(4,128)S(1)} %iota_add_fusion, bf16[4,1,2,64,64]{4,3,2,1,0:T(8,128)(2,1)S(1)} %reshape.306), kind=kOutput, calls=%fused_computation.12 | convolution fusion | flops 9568256 | bytes 460800 | tf_op jit(solution)/shard_map/fkuv,fav->fkua/dot_general | solution.py:60
  42.2 1.2 %convolution_bitcast_fusion = f32[256,256]{1,0:T(8,128)S(1)} fusion(bf16[4,64,256]{2,1,0:T(8,128)(2,1)S(1)} %fusion.6, s32[4,64]{1,0:T(4,128)S(1)} %iota_add_fusion), kind=kOutput, calls=%fused_computation.2 | convolution fusion | flops 34603008 | bytes 394240 | tf_op jit(solution)/shard_map/fau,fkub->kab/dot_general | solution.py:60
  43.4 1.2 %fusion.2 = f32[1,256,256]{1,2,0:T(8,128)S(1)} fusion(f32[256,256]{1,0:T(8,128)S(1)} %convolution_bitcast_fusion.2, bf16[4,64,256]{2,1,0:T(8,128)(2,1)S(1)} %fusion.6, s32[4,64]{1,0:T(4,128)S(1)} %iota_add_fusion), kind=kOutput, calls=%fused_computation.8 | convolution fusion | flops 34734080 | bytes 656384 | tf_op jit(solution)/shard_map/fau,fkub->kab/dot_general | solution.py:60
  44.6 1.2 %fusion.30 = (bf16[256,256]{0,1:T(8,128)(2,1)S(1)}, bf16[256,256]{0,1:T(8,128)(2,1)S(1)}) fusion(f32[1,2,256,256]{2,3,1,0:T(8,128)S(1)} %broadcast_select_fusion, f32[1,256,256]{1,2,0:T(8,128)S(1)} %fusion.2, f32[256,256]{1,0:T(8,128)S(1)} %convolution_bitcast_fusion, bf16[4,64,256]{2,1,0:T(8,128)(2,1)S(1)} %fusion.7, s32[4,64]{1,0:T(4,128)S(1)} %iota_add_fusion), kind=kOutput, calls=%fused_computation.63 | convolution fusion | flops 35258368 | bytes 1442816 | tf_op jit(solution)/shard_map/fau,fkub->kab/dot_general | solution.py:60
  46.8 1.4 %fusion.38 = f32[4,64,64]{2,1,0:T(8,128)S(1)} fusion(bf16[4,64,256]{2,1,0:T(8,128)(2,1)S(1)} %fusion.31, s32[4,64]{1,0:T(4,128)S(1)} %iota_add_fusion), kind=kOutput, calls=%fused_computation.77 | convolution fusion | flops 9633792 | bytes 197632 | tf_op jit(solution)/shard_map/fkub,fbv->fkuv/dot_general | solution.py:60
  48.2 1.4 %fusion.35 = f32[4,64,64]{2,1,0:T(8,128)S(1)} fusion(bf16[4,64,256]{2,1,0:T(8,128)(2,1)S(1)} %fusion.31, s32[4,64]{1,0:T(4,128)S(1)} %iota_add_fusion), kind=kOutput, calls=%fused_computation.70 | convolution fusion | flops 9437184 | bytes 197632 | tf_op jit(solution)/shard_map/fkub,fbv->fkuv/dot_general | solution.py:60
  49.7 1.2 %fusion.10 = bf16[4,1,1,64,64]{4,3,0,2,1:T(8,128)(2,1)S(1)} fusion(f32[4,64,64]{2,1,0:T(8,128)S(1)} %fusion.38, bf16[4,64,256]{2,1,0:T(8,128)(2,1)S(1)} %fusion.32, s32[4,64]{1,0:T(4,128)S(1)} %iota_add_fusion), kind=kOutput, calls=%fused_computation.20 | convolution fusion | flops 9469952 | bytes 230400 | tf_op jit(solution)/shard_map/fkub,fbv->fkuv/dot_general | solution.py:60
  50.9 1.2 %fusion.11 = bf16[4,1,1,64,64]{4,3,0,2,1:T(8,128)(2,1)S(1)} fusion(f32[4,64,64]{2,1,0:T(8,128)S(1)} %fusion.35, bf16[4,64,256]{2,1,0:T(8,128)(2,1)S(1)} %fusion.32, s32[4,64]{1,0:T(4,128)S(1)} %iota_add_fusion), kind=kOutput, calls=%fused_computation.21 | convolution fusion | flops 9666560 | bytes 230400 | tf_op jit(solution)/shard_map/fkub,fbv->fkuv/dot_general | solution.py:60
  52.3 8.1 %all_to_all.10 = bf16[4,2,4096]{2,1,0:T(2,128)(2,1)S(1)} all-to-all(bf16[4,2,4096]{2,1,0:T(2,128)(2,1)S(1)} %reshape.307), channel_id=1, replica_groups=mesh['facet'=4,'col'=8] {'facet'}, dimensions={0} | all-to-all | bytes 131072 | tf_op jit(solution)/shard_map/all_to_all | solution.py:119
  60.5 0.7 fusion.46
  61.3 0.7 fusion.45
  62.0 0.7 fusion.18
  63.5 0.7 fusion.19
  65.0 0.6 pad_maximum_fusion.2
  65.7 29.2 %reduce-scatter.2.cloned.1.call-done = f32[8,2,128]{2,0,1:T(8,128)} async-done(((f32[64,2,128]{2,0,1:T(8,128)}), f32[8,2,128]{2,0,1:T(8,128)}) %reduce-scatter.2.cloned.1.call-update) | async-done | bytes 8208 | tf_op jit(solution)/shard_map/reduce_scatter | solution.py:129
  94.8 0.7 multiply_bitcast_fusion
  (37 shorter events, 6.1 us)
Async XLA Ops:
  6.5 23.8 %copy-start = (f32[4,2,256,256]{3,2,1,0:T(8,128)S(1)}, f32[4,2,256,256]{3,2,1,0:T(8,128)}, u32[]{:S(2)}) copy-start(f32[4,2,256,256]{3,2,1,0:T(8,128)} %param.9) | copy-start | bytes 6291460
  24.8 10.6 %all-to-all-start = ((bf16[4,2,4096]{2,1,0:T(2,128)(2,1)}), bf16[4,2,4096]{2,1,0:T(2,128)(2,1)S(1)}, u32[]{:S(2)}, u32[]{:S(2)}) async-start(bf16[4,2,4096]{2,1,0:T(2,128)(2,1)} %reshape.305), calls=%async_computation | async-start | bytes 131072 | tf_op jit(solution)/shard_map/all_to_all | solution.py:98
  29.6 65.2 %reduce-scatter.2.cloned.1.call-start = ((), (), s32[]{:S(2)}) async-start(), calls=%async_computation.3 | async-start | bytes 73728 | tf_op jit(solution)/shard_map/reduce_scatter | solution.py:129
Sparse Core Ops, SparseCore 0:
  65.8 28.9 reduce-scatter.1
where the time goes:
time: 103 us
  waiting for transfers between devices  31.7 us (31%)
  matrix products  25.2 us (24%)
  blocking collectives  18.4 us (18%)
  between operations  15.1 us (15%)
  starting transfers between devices  4.87 us (5%)
  other arithmetic  4.49 us (4%)
  local copies, waits for them, and re-layouts  3.13 us (3%)
    reduce_scatter x1, waiting for transfers between devices, body(): lax.psum_scatter(jnp.stack([summand[0], summand[1]], axis=1), 'col', scat...  29.2 us
    dot_general x12, matrix products, single(): jnp.einsum(form, left_part, right_part, preferred_element_type=jnp.float32)  15.4 us
    all_gather x1, blocking collectives, body(): whole_slab = lax.all_gather(facets[0], 'col', axis=0, tiled=True)  10.3 us
    dot_general x16, matrix products, general_dot(): lax.dot_general(first_op, second_op, numbers, preferred_element_type=jnp....  8.9 us
    all_to_all x1, blocking collectives, body(): lax.all_to_all(going_back, 'facet', split_axis=0, concat_axis=0, tiled=True)  8.11 us
    all_to_all x1, starting transfers between devices, body(): lax.all_to_all(outgoing, 'facet', split_axis=0, concat_axis=0, tiled=True)  4.87 us
    all_to_all x1, waiting for transfers between devices, body(): lax.all_to_all(outgoing, 'facet', split_axis=0, concat_axis=0, tiled=True)  2.54 us
    unnamed x8, local copies, waits for them, and re-layouts  2.12 us
  transfers between devices with their start and end apart: 2, of which 2 were waited for; matrix products, arithmetic and copies ran while one was open for 2% of the time, Pallas kernels for 0%

commit v1 on v0

--- a/solution.py
+++ b/solution.py
@@ -84,7 +84,9 @@
     )
     embedding = embed_table(jnp.arange(facet_count, dtype=jnp.int32))
     adjoint_embed = (embedding[0], -embedding[1])
-    whole_slab = lax.all_gather(facets[0], "col", axis=0, tiled=True)
+    block = facets[0]
+    sent = jnp.stack([block] * lax.axis_size("col"))
+    whole_slab = jnp.concatenate(lax.all_to_all(sent, "col", 0, 0), axis=0)
     spread = round_pair(complex_dot((whole_slab[:, 0], whole_slab[:, 1]), across, ((1,), (0,))))
     block_phase = (row_flat[0], row_flat[1])
     summand = complex_dot(block_phase, spread, ((1,), (0,)))

time: 103 us -> 102 us (level)
  blocking collectives: 18.4 us -> 8.11 us
  starting transfers between devices: 4.87 us -> 10.1 us
  waiting for transfers between devices: 31.7 us -> 35.3 us
    all_gather x1 -> x0, blocking collectives: 10.3 us -> none  [body(): whole_slab = lax.all_gather(facets[0], 'col', axis=0, tiled=True)]
    all_to_all x0 -> x1, starting transfers between devices: none -> 5.2 us  [body(): whole_slab = jnp.concatenate(lax.all_to_all(sent, 'col', 0, 0), axis=0)]
    all_to_all x1, waiting for transfers between devices: 2.54 us -> 4.67 us  [body(): lax.all_to_all(outgoing, 'facet', split_axis=0, concat_axis=0, tiled=True)]
    all_to_all x0 -> x1, waiting for transfers between devices: none -> 1.85 us  [body(): whole_slab = jnp.concatenate(lax.all_to_all(sent, 'col', 0, 0), axis=0)]
    another operation x0 -> x2, local copies, waits for them, and re-layouts: none -> 1.45 us
    unnamed x8 -> x9, local copies, waits for them, and re-layouts: 2.12 us -> 1.45 us
  transfers between devices with their start and end apart: 2 -> 3, of which waited for: 2 -> 3; matrix products, arithmetic and copies ran while one was open for 2% -> 3% of each run, Pallas kernels for 0% -> 0%
where the time goes in v1:
time: 102 us; the launch traced here: 101 us
  waiting for transfers between devices  35.3 us (35%)
  matrix products  25.2 us (25%)
  between operations  15 us (15%)
  starting transfers between devices  10.1 us (10%)
  blocking collectives  8.11 us (8%)
  local copies, waits for them, and re-layouts  3.91 us (4%)
  other arithmetic  3.84 us (4%)
    reduce_scatter x1, waiting for transfers between devices, body(): lax.psum_scatter(jnp.stack([summand[0], summand[1]], axis=1), 'col', scat...  28.8 us
    dot_general x12, matrix products, single(): jnp.einsum(form, left_part, right_part, preferred_element_type=jnp.float32)  15.4 us
    dot_general x16, matrix products, general_dot(): lax.dot_general(first_op, second_op, numbers, preferred_element_type=jnp....  8.91 us
    all_to_all x1, blocking collectives, body(): lax.all_to_all(going_back, 'facet', split_axis=0, concat_axis=0, tiled=True)  8.11 us
    all_to_all x1, starting transfers between devices, body(): whole_slab = jnp.concatenate(lax.all_to_all(sent, 'col', 0, 0), axis=0)  5.2 us
    all_to_all x1, starting transfers between devices, body(): lax.all_to_all(outgoing, 'facet', split_axis=0, concat_axis=0, tiled=True)  4.87 us
    all_to_all x1, waiting for transfers between devices, body(): lax.all_to_all(outgoing, 'facet', split_axis=0, concat_axis=0, tiled=True)  4.67 us
  transfers between devices with their start and end apart: 3, of which 3 were waited for; matrix products, arithmetic and copies ran while one was open for 3% of the time, Pallas kernels for 0%

profile of v1, /device:TPU:0, one launch (start us, length us, event | category | flops | bytes accessed | tf_op | source)
XLA Modules:
  0.0 101.5 jit_solution(10599858393245978030)
XLA Ops:
  6.5 0.8 copy.23
  8.0 5.2 %all-to-all-start = ((bf16[8,8,2,128]{3,1,2,0:T(8,128)(2,1)}), bf16[8,8,2,128]{3,1,2,0:T(8,128)(2,1)S(1)}, u32[]{:S(2)}, u32[]{:S(2)}) async-start(bf16[8,8,2,128]{3,1,2,0:T(8,128)(2,1)} %stack.31), calls=%async_computation | async-start | bytes 65536 | tf_op jit(solution)/shard_map/all_to_all | solution.py:89
  15.0 1.1 %multiply_convert_fusion.1 = bf16[4,256,64]{1,2,0:T(8,128)(2,1)S(1)} fusion(s32[4,64]{1,0:T(4,128)S(1)} %iota_add_fusion), kind=kLoop, calls=%fused_computation.50 | loop fusion | flops 1048576 | bytes 132096 | tf_op jit(solution)/shard_map/convert_element_type | solution.py:16
  16.2 1.9 %all-to-all-done = bf16[8,8,2,128]{3,1,2,0:T(8,128)(2,1)S(1)} async-done(((bf16[8,8,2,128]{3,1,2,0:T(8,128)(2,1)}), bf16[8,8,2,128]{3,1,2,0:T(8,128)(2,1)S(1)}, u32[]{:S(2)}, u32[]{:S(2)}) %all-to-all-start) | async-done | bytes 32800 | tf_op jit(solution)/shard_map/all_to_all | solution.py:89
  19.7 0.7 fusion.47
  20.4 0.7 fusion.48
  21.1 0.7 fusion.13
  21.9 0.7 fusion.12
  22.8 0.8 reshape.309
  23.6 4.9 %all-to-all-start.1 = ((bf16[4,2,4096]{2,1,0:T(2,128)(2,1)}), bf16[4,2,4096]{2,1,0:T(2,128)(2,1)S(1)}, u32[]{:S(2)}, u32[]{:S(2)}) async-start(bf16[4,2,4096]{2,1,0:T(2,128)(2,1)} %reshape.309), calls=%async_computation.1 | async-start | bytes 131072 | tf_op jit(solution)/shard_map/all_to_all | solution.py:100
  28.5 1.1 %fusion.33 = bf16[4,256,64]{1,2,0:T(8,128)(2,1)S(1)} fusion(s32[4,64]{1,0:T(4,128)S(1)} %iota_add_fusion), kind=kLoop, calls=%fused_computation.68 | loop fusion | flops 1245184 | bytes 132096 | tf_op jit(solution)/shard_map/neg | solution.py:86
  29.6 4.7 %all-to-all-done.1 = bf16[4,2,4096]{2,1,0:T(2,128)(2,1)S(1)} async-done(((bf16[4,2,4096]{2,1,0:T(2,128)(2,1)}), bf16[4,2,4096]{2,1,0:T(2,128)(2,1)S(1)}, u32[]{:S(2)}, u32[]{:S(2)}) %all-to-all-start.1) | async-done | bytes 65568 | tf_op jit(solution)/shard_map/all_to_all | solution.py:100
  34.4 1.6 %fusion.34 = f32[4,64,256]{2,1,0:T(8,128)S(1)} fusion(s32[4,64]{1,0:T(4,128)S(1)} %iota_add_fusion, bf16[4,1,2,64,64]{4,3,2,1,0:T(8,128)(2,1)S(1)} %reshape.310), kind=kOutput, calls=%fused_computation.69 | convolution fusion | flops 9437184 | bytes 329728 | tf_op jit(solution)/shard_map/fkuv,fav->fkua/dot_general | solution.py:60
  36.0 1.4 %fusion.36 = f32[4,64,256]{2,1,0:T(8,128)S(1)} fusion(s32[4,64]{1,0:T(4,128)S(1)} %iota_add_fusion, bf16[4,1,2,64,64]{4,3,2,1,0:T(8,128)(2,1)S(1)} %reshape.310), kind=kOutput, calls=%fused_computation.71 | convolution fusion | flops 9437184 | bytes 329728 | tf_op jit(solution)/shard_map/fkuv,fav->fkua/dot_general | solution.py:60
  37.4 1.2 %fusion.7 = bf16[4,64,256]{2,1,0:T(8,128)(2,1)S(1)} fusion(f32[4,64,256]{2,1,0:T(8,128)S(1)} %fusion.34, s32[4,64]{1,0:T(4,128)S(1)} %iota_add_fusion, bf16[4,1,2,64,64]{4,3,2,1,0:T(8,128)(2,1)S(1)} %reshape.310), kind=kOutput, calls=%fused_computation.13 | convolution fusion | flops 9568256 | bytes 460800 | tf_op jit(solution)/shard_map/fkuv,fav->fkua/dot_general | solution.py:60
  38.6 1.2 %convolution_bitcast_fusion.2 = f32[256,256]{1,0:T(8,128)S(1)} fusion(bf16[4,64,256]{2,1,0:T(8,128)(2,1)S(1)} %fusion.7, s32[4,64]{1,0:T(4,128)S(1)} %iota_add_fusion), kind=kOutput, calls=%fused_computation.4 | convolution fusion | flops 34603008 | bytes 394240 | tf_op jit(solution)/shard_map/fau,fkub->kab/dot_general | solution.py:60
  39.8 1.2 %fusion.6 = bf16[4,64,256]{2,1,0:T(8,128)(2,1)S(1)} fusion(f32[4,64,256]{2,1,0:T(8,128)S(1)} %fusion.36, s32[4,64]{1,0:T(4,128)S(1)} %iota_add_fusion, bf16[4,1,2,64,64]{4,3,2,1,0:T(8,128)(2,1)S(1)} %reshape.310), kind=kOutput, calls=%fused_computation.12 | convolution fusion | flops 9568256 | bytes 460800 | tf_op jit(solution)/shard_map/fkuv,fav->fkua/dot_general | solution.py:60
  41.0 1.2 %convolution_bitcast_fusion = f32[256,256]{1,0:T(8,128)S(1)} fusion(bf16[4,64,256]{2,1,0:T(8,128)(2,1)S(1)} %fusion.6, s32[4,64]{1,0:T(4,128)S(1)} %iota_add_fusion), kind=kOutput, calls=%fused_computation.2 | convolution fusion | flops 34603008 | bytes 394240 | tf_op jit(solution)/shard_map/fau,fkub->kab/dot_general | solution.py:60
  42.2 1.2 %fusion.2 = f32[1,256,256]{1,2,0:T(8,128)S(1)} fusion(f32[256,256]{1,0:T(8,128)S(1)} %convolution_bitcast_fusion.2, bf16[4,64,256]{2,1,0:T(8,128)(2,1)S(1)} %fusion.6, s32[4,64]{1,0:T(4,128)S(1)} %iota_add_fusion), kind=kOutput, calls=%fused_computation.8 | convolution fusion | flops 34734080 | bytes 656384 | tf_op jit(solution)/shard_map/fau,fkub->kab/dot_general | solution.py:60
  43.4 1.2 %fusion.30 = (bf16[256,256]{0,1:T(8,128)(2,1)S(1)}, bf16[256,256]{0,1:T(8,128)(2,1)S(1)}) fusion(f32[1,2,256,256]{2,3,1,0:T(8,128)S(1)} %broadcast_select_fusion, f32[1,256,256]{1,2,0:T(8,128)S(1)} %fusion.2, f32[256,256]{1,0:T(8,128)S(1)} %convolution_bitcast_fusion, bf16[4,64,256]{2,1,0:T(8,128)(2,1)S(1)} %fusion.7, s32[4,64]{1,0:T(4,128)S(1)} %iota_add_fusion), kind=kOutput, calls=%fused_computation.63 | convolution fusion | flops 35258368 | bytes 1442816 | tf_op jit(solution)/shard_map/fau,fkub->kab/dot_general | solution.py:60
  45.6 1.4 %fusion.38 = f32[4,64,64]{2,1,0:T(8,128)S(1)} fusion(bf16[4,64,256]{2,1,0:T(8,128)(2,1)S(1)} %fusion.31, s32[4,64]{1,0:T(4,128)S(1)} %iota_add_fusion), kind=kOutput, calls=%fused_computation.77 | convolution fusion | flops 9633792 | bytes 197632 | tf_op jit(solution)/shard_map/fkub,fbv->fkuv/dot_general | solution.py:60
  47.0 1.4 %fusion.35 = f32[4,64,64]{2,1,0:T(8,128)S(1)} fusion(bf16[4,64,256]{2,1,0:T(8,128)(2,1)S(1)} %fusion.31, s32[4,64]{1,0:T(4,128)S(1)} %iota_add_fusion), kind=kOutput, calls=%fused_computation.70 | convolution fusion | flops 9437184 | bytes 197632 | tf_op jit(solution)/shard_map/fkub,fbv->fkuv/dot_general | solution.py:60
  48.5 1.2 %fusion.10 = bf16[4,1,1,64,64]{4,3,0,2,1:T(8,128)(2,1)S(1)} fusion(f32[4,64,64]{2,1,0:T(8,128)S(1)} %fusion.38, bf16[4,64,256]{2,1,0:T(8,128)(2,1)S(1)} %fusion.32, s32[4,64]{1,0:T(4,128)S(1)} %iota_add_fusion), kind=kOutput, calls=%fused_computation.20 | convolution fusion | flops 9469952 | bytes 230400 | tf_op jit(solution)/shard_map/fkub,fbv->fkuv/dot_general | solution.py:60
  49.7 1.2 %fusion.11 = bf16[4,1,1,64,64]{4,3,0,2,1:T(8,128)(2,1)S(1)} fusion(f32[4,64,64]{2,1,0:T(8,128)S(1)} %fusion.35, bf16[4,64,256]{2,1,0:T(8,128)(2,1)S(1)} %fusion.32, s32[4,64]{1,0:T(4,128)S(1)} %iota_add_fusion), kind=kOutput, calls=%fused_computation.21 | convolution fusion | flops 9666560 | bytes 230400 | tf_op jit(solution)/shard_map/fkub,fbv->fkuv/dot_general | solution.py:60
  51.1 8.1 %all_to_all.15 = bf16[4,2,4096]{2,1,0:T(2,128)(2,1)S(1)} all-to-all(bf16[4,2,4096]{2,1,0:T(2,128)(2,1)S(1)} %reshape.311), channel_id=1, replica_groups=mesh['facet'=4,'col'=8] {'facet'}, dimensions={0} | all-to-all | bytes 131072 | tf_op jit(solution)/shard_map/all_to_all | solution.py:121
  59.4 0.7 fusion.46
  60.1 0.7 fusion.45
  60.8 0.7 fusion.18
  62.4 0.7 fusion.19
  63.9 0.6 pad_maximum_fusion.2
  64.5 28.8 %reduce-scatter.2.cloned.1.call-done = f32[8,2,128]{2,0,1:T(8,128)} async-done(((f32[64,2,128]{2,0,1:T(8,128)}), f32[8,2,128]{2,0,1:T(8,128)}) %reduce-scatter.2.cloned.1.call-update) | async-done | bytes 8208 | tf_op jit(solution)/shard_map/reduce_scatter | solution.py:131
  93.3 0.7 multiply_bitcast_fusion
  (42 shorter events, 6.8 us)
Async XLA Ops:
  6.5 7.3 %copy-start = (f32[4,2,256,256]{3,2,1,0:T(8,128)S(1)}, f32[4,2,256,256]{3,2,1,0:T(8,128)}, u32[]{:S(2)}) copy-start(f32[4,2,256,256]{3,2,1,0:T(8,128)} %param.9) | copy-start | bytes 6291460
  6.5 8.3 %copy-start.1 = (s32[1,4]{1,0:T(1,128)S(1)}, s32[1,4]{1,0:T(1,128)}, u32[]{:S(2)}) copy-start(s32[1,4]{1,0:T(1,128)} %param.6) | copy-start | bytes 52
  8.0 10.0 %all-to-all-start = ((bf16[8,8,2,128]{3,1,2,0:T(8,128)(2,1)}), bf16[8,8,2,128]{3,1,2,0:T(8,128)(2,1)S(1)}, u32[]{:S(2)}, u32[]{:S(2)}) async-start(bf16[8,8,2,128]{3,1,2,0:T(8,128)(2,1)} %stack.31), calls=%async_computation | async-start | bytes 65536 | tf_op jit(solution)/shard_map/all_to_all | solution.py:89
  23.6 10.6 %all-to-all-start.1 = ((bf16[4,2,4096]{2,1,0:T(2,128)(2,1)}), bf16[4,2,4096]{2,1,0:T(2,128)(2,1)S(1)}, u32[]{:S(2)}, u32[]{:S(2)}) async-start(bf16[4,2,4096]{2,1,0:T(2,128)(2,1)} %reshape.309), calls=%async_computation.1 | async-start | bytes 131072 | tf_op jit(solution)/shard_map/all_to_all | solution.py:100
  28.5 64.8 %reduce-scatter.2.cloned.1.call-start = ((), (), s32[]{:S(2)}) async-start(), calls=%async_computation.4 | async-start | bytes 73728 | tf_op jit(solution)/shard_map/reduce_scatter | solution.py:131
Sparse Core Ops, SparseCore 0:
  64.7 28.6 reduce-scatter.1
